TPU v7x, 128 devices: a whole 4x4x4 slice. The times are simulated.
128 devices in a mesh: row: 16 (over y, x_lo, core), col: 8 (over z, x_hi).
Axes of the slice: x: 4 (x_hi: 2, x_lo: 2; x = x_hi * 2 + x_lo), y: 4, z: 4, core: 2. Of those that a mesh axis runs over, the one named last changes fastest.
Arguments:
- features: float32 [65536, 256], P(('col', 'row')), may hold values from -6 to 6
- weight_matrix: float32 [256, 256], replicated, may hold values from -0.375 to 0.375
- cotangent: float32 [65536, 256], P(('row', 'col')), may hold values from -6 to 6
- block_rows: int32 [16, 8, 96], P('row', 'col'), may hold values from 0 to 31
- block_cols: int32 [16, 8, 96], P('row', 'col'), may hold values from 0 to 63
- blocks: float32 [16, 8, 96, 128, 128], P('row', 'col'), may hold values from -0.109375 to 0.109375
Outputs:
- hidden: float32 [65536, 256], P(('row', 'col'))
- weight_grad: float32 [256, 256], replicated
- feature_grad: float32 [65536, 256], P(('col', 'row'))
All inputs are finite; a program needn't handle non-finite values.
Results may differ from a plain program's by a relative error of at most 0.0001.
Values sent between devices are 32-bit elements; how exact they have to be, the bound alone decides.
A program may use at most 128 MiB of HBM per device.

v0:
```python
import jax
import jax.numpy as jnp
from jax import lax
from jax.sharding import PartitionSpec as P


def activate(pre, cotangent):
    sigmoid_v = 1.0 / (1.0 + jnp.exp(-pre))
    return (pre * sigmoid_v, cotangent * sigmoid_v * (1.0 + pre * (1.0 - sigmoid_v)))


def tile_product(values, take_ids, put_ids, source, put_count, form):
    size_block = values.shape[-1]
    width = source.shape[1]
    chosen = source.reshape(-1, size_block, width)[take_ids]
    products = jnp.einsum(form, values, chosen, precision=lax.Precision.HIGHEST)
    summed = jnp.zeros((put_count, size_block, width), jnp.float32).at[put_ids].add(products)
    return summed.reshape(put_count * size_block, width)


def shards(features, weight_matrix, cotangent, block_rows, block_cols, blocks):
    high = lax.Precision.HIGHEST
    tile_values = blocks[0, 0]
    rows_here = block_rows[0, 0]
    cols_here = block_cols[0, 0]
    size_block = tile_values.shape[-1]
    rows_dev = features.shape[0]
    count_row = lax.axis_size("row")
    count_col = lax.axis_size("col")
    row_blocks = rows_dev * count_col // size_block
    col_blocks = rows_dev * count_row // size_block
    total_nodes = rows_dev * count_row * count_col
    feature_tile = lax.all_gather(features, "row", axis=0, tiled=True)
    partial_value = tile_product(
        tile_values, cols_here, rows_here, feature_tile, row_blocks, "kij,kjf->kif"
    )
    own_inputs = lax.psum_scatter(partial_value, "col", scatter_dimension=0, tiled=True)
    pre = jnp.dot(own_inputs, weight_matrix, precision=high)
    hidden, own_dpre = activate(pre, cotangent)
    back_own = jnp.dot(own_dpre, weight_matrix.T, precision=high)
    back_rows = lax.all_gather(back_own, "col", axis=0, tiled=True)
    local_grad = lax.dot_general(own_inputs, own_dpre, (((0,), (0,)), ((), ())), precision=high)
    local_grad = local_grad / jnp.sqrt(jnp.float32(total_nodes))
    weight_grad = lax.psum(local_grad, ("row", "col"))
    grad_part = tile_product(
        tile_values, rows_here, cols_here, back_rows, col_blocks, "kji,kjf->kif"
    )
    feature_grad = lax.psum_scatter(grad_part, "row", scatter_dimension=0, tiled=True)
    return (hidden, weight_grad, feature_grad)


def solution(mesh):
    in_specs = (
        P(("col", "row"), None),
        P(),
        P(("row", "col"), None),
        P("row", "col", None),
        P("row", "col", None),
        P("row", "col", None, None, None),
    )
    out_specs = (P(("row", "col"), None), P(), P(("col", "row"), None))
    return jax.shard_map(shards, mesh=mesh, in_specs=in_specs, out_specs=out_specs, check_vma=False)
```

profile of v0, /device:TPU:0, one launch (start us, length us, event | category | flops | bytes accessed | tf_op | source)
XLA Modules:
  0.0 558.9 jit_solution(4916594106256238890)
XLA Ops:
  7.2 0.0 copy-start
  7.2 0.0 all-gather.3.cloned.1.call-start
  7.2 0.7 all-gather.3.cloned.1.call-update
  7.9 0.0 reduce-scatter.3.cloned.1.call-start
  8.0 0.7 fusion.12
  8.6 0.7 fusion.11
  9.3 55.0 %all-gather.3.cloned.1.call-done = f32[8192,256]{1,0:T(8,128)} async-done(((f32[512,256]{1,0:T(8,128)}), f32[8192,256]{1,0:T(8,128)}) %all-gather.3.cloned.1.call-update) | async-done | bytes 8388624 | tf_op jit(solution)/shard_map/all_gather | solution.py:33
  64.2 12.1 %gather_fusion = f32[96,128,256]{2,1,0:T(8,128)} fusion(f32[64,128,256]{2,1,0:T(8,128)} %bitcast.34, s32[1024]{0:T(1024)S(1)} %pad_clamp_fusion.1), kind=kCustom, calls=%fused_computation | custom fusion | bytes 25166208 | tf_op jit(solution)/shard_map/gather | solution.py:15
  76.3 27.0 %fusion.4 = f32[96,128,256]{1,2,0:T(8,128)} fusion(f32[96,128,256]{2,1,0:T(8,128)} %gather_fusion, f32[1,1,96,128,128]{4,3,2,1,0:T(8,128)} %param.11), kind=kOutput, calls=%fused_computation.8 | convolution fusion | flops 4831838208 | bytes 31457280 | tf_op jit(solution)/shard_map/kij,kjf->kif/dot_general | solution.py:16
  103.3 12.6 %copy.12 = f32[96,128,256]{2,1,0:T(8,128)} copy(f32[96,128,256]{1,2,0:T(8,128)} %fusion.4) | data formatting | bytes 25165824 | tf_op jit(solution)/shard_map/kij,kjf->kif/dot_general | solution.py:16
  115.9 2.4 broadcast_in_dim.4
  118.3 27.8 %scatter_fusion = f32[32,128,256]{2,1,0:T(8,128)} fusion(f32[32,128,256]{2,1,0:T(8,128)} %broadcast_in_dim.4, s32[96]{0:T(128)S(1)} %fusion.11, f32[96,128,256]{2,1,0:T(8,128)} %copy.12), kind=kCustom, calls=%fused_computation.2 | custom fusion | flops 3145728 | bytes 37749120 | tf_op jit(solution)/shard_map/scatter-add | solution.py:17
  146.1 0.0 reduce-scatter.3.cloned.1.call-update
  146.1 0.2 all-gather.5.cloned.1.call-start
  146.3 86.1 %reduce-scatter.3.cloned.1.call-done = f32[512,256]{1,0:T(8,128)} async-done(((f32[4096,256]{1,0:T(8,128)}), f32[512,256]{1,0:T(8,128)}) %reduce-scatter.3.cloned.1.call-update) | async-done | bytes 524304 | tf_op jit(solution)/shard_map/reduce_scatter | solution.py:37
  232.4 2.4 fusion.10
  234.9 1.5 fusion.13
  236.4 0.0 all-gather.5.cloned.1.call-update
  236.4 0.0 all-reduce.2.cloned.1.call-start
  236.5 2.8 convolution_multiply_fusion
  239.3 0.0 all-reduce.2.cloned.1.call-update
  239.4 0.0 reduce-scatter.5.cloned.1.call-start
  239.4 67.2 %all-gather.5.cloned.1.call-done = f32[4096,256]{1,0:T(8,128)} async-done(((f32[512,256]{1,0:T(8,128)}), f32[4096,256]{1,0:T(8,128)}) %all-gather.5.cloned.1.call-update) | async-done | bytes 4194320 | tf_op jit(solution)/shard_map/all_gather | solution.py:41
  306.6 10.8 %gather_fusion.1 = f32[96,128,256]{2,1,0:T(8,128)} fusion(f32[32,128,256]{2,1,0:T(8,128)} %bitcast.33, s32[1024]{0:T(1024)S(1)} %pad_clamp_fusion), kind=kCustom, calls=%fused_computation.1 | custom fusion | bytes 25166208 | tf_op jit(solution)/shard_map/gather | solution.py:15
  317.5 26.9 %fusion.7 = f32[96,128,256]{1,2,0:T(8,128)} fusion(f32[96,128,256]{2,1,0:T(8,128)} %gather_fusion.1, f32[1,1,96,128,128]{4,3,2,1,0:T(8,128)} %param.11), kind=kOutput, calls=%fused_computation.9 | convolution fusion | flops 4831838208 | bytes 31457280 | tf_op jit(solution)/shard_map/kji,kjf->kif/dot_general | solution.py:16
  344.4 12.6 %copy.14 = f32[96,128,256]{2,1,0:T(8,128)} copy(f32[96,128,256]{1,2,0:T(8,128)} %fusion.7) | data formatting | bytes 25165824 | tf_op jit(solution)/shard_map/kji,kjf->kif/dot_general | solution.py:16
  357.0 4.2 broadcast_in_dim.5
  361.2 29.0 %scatter_fusion.1 = f32[64,128,256]{2,1,0:T(8,128)} fusion(f32[64,128,256]{2,1,0:T(8,128)} %broadcast_in_dim.5, s32[96]{0:T(128)S(1)} %fusion.12, f32[96,128,256]{2,1,0:T(8,128)} %copy.14), kind=kCustom, calls=%fused_computation.3 | custom fusion | flops 3145728 | bytes 37749120 | tf_op jit(solution)/shard_map/scatter-add | solution.py:17
  390.2 0.0 reduce-scatter.5.cloned.1.call-update
  390.2 62.6 %all-reduce.2.cloned.1.call-done = f32[256,256]{1,0:T(8,128)} async-done(((f32[256,256]{1,0:T(8,128)}), f32[256,256]{1,0:T(8,128)}) %all-reduce.2.cloned.1.call-update) | async-done | bytes 262160 | tf_op jit(solution)/shard_map/psum | solution.py:44
  452.8 97.9 %reduce-scatter.5.cloned.1.call-done = f32[512,256]{1,0:T(8,128)} async-done(((f32[8192,256]{1,0:T(8,128)}), f32[512,256]{1,0:T(8,128)}) %reduce-scatter.5.cloned.1.call-update) | async-done | bytes 524304 | tf_op jit(solution)/shard_map/reduce_scatter | solution.py:48
  550.7 1.7 copy.20
  (7 shorter events, 0.0 us)
Async XLA Ops:
  7.2 225.3 %copy-start = (f32[256,256]{1,0:T(8,128)S(1)}, f32[256,256]{1,0:T(8,128)}, u32[]{:S(2)}) copy-start(f32[256,256]{1,0:T(8,128)} %param.7) | copy-start | bytes 786436
  7.2 57.1 %all-gather.3.cloned.1.call-start = ((), (), s32[]{:S(2)}) async-start(), calls=%async_computation.2 | async-start | bytes 8912896 | tf_op jit(solution)/shard_map/all_gather | solution.py:33
  7.9 224.5 %reduce-scatter.3.cloned.1.call-start = ((), (), s32[]{:S(2)}) async-start(), calls=%async_computation.3 | async-start | bytes 4718592 | tf_op jit(solution)/shard_map/reduce_scatter | solution.py:37
  118.3 116.6 %copy-start.2 = (f32[512,256]{1,0:T(8,128)S(1)}, f32[512,256]{1,0:T(8,128)}, u32[]{:S(2)}) copy-start(f32[512,256]{1,0:T(8,128)} %param.8) | copy-start | bytes 1572868
  146.1 160.5 %all-gather.5.cloned.1.call-start = ((), (), s32[]{:S(2)}) async-start(), calls=%async_computation.5 | async-start | bytes 4718592 | tf_op jit(solution)/shard_map/all_gather | solution.py:41
  236.4 216.4 %all-reduce.2.cloned.1.call-start = ((), (), s32[]{:S(2)}) async-start(), calls=%async_computation.4 | async-start | bytes 524288 | tf_op jit(solution)/shard_map/psum | solution.py:44
  239.4 311.4 %reduce-scatter.5.cloned.1.call-start = ((), (), s32[]{:S(2)}) async-start(), calls=%async_computation.6 | async-start | bytes 8912896 | tf_op jit(solution)/shard_map/reduce_scatter | solution.py:48
  361.2 191.2 %copy-start.1 = (f32[256,256]{1,0:T(8,128)S(1)}, f32[256,256]{1,0:T(8,128)}, u32[]{:S(2)}) copy-start(f32[256,256]{1,0:T(8,128)} %param.7) | copy-start | bytes 786436
Sparse Core Ops, SparseCore 0:
  9.7 54.5 all-gather.2
  146.2 86.1 reduce-scatter.2
  236.6 70.0 all-gather.4
  311.8 140.9 all-reduce.1
  455.7 95.0 reduce-scatter.4
where the time goes:
time: 560 us; the launch traced here: 559 us
  waiting for transfers between devices  370 us (66%)
  matrix products  60.7 us (11%)
  other arithmetic  58.1 us (10%)
  local copies, waits for them, and re-layouts  56.4 us (10%)
  between operations  13.8 us (2%)
    reduce_scatter x1, waiting for transfers between devices, shards(): lax.psum_scatter(grad_part, 'row', scatter_dimension=0, tiled=True)  97.9 us
    reduce_scatter x1, waiting for transfers between devices, shards(): lax.psum_scatter(partial_value, 'col', scatter_dimension=0, tiled=True)  86.1 us
    all_gather x1, waiting for transfers between devices, shards(): back_rows = lax.all_gather(back_own, 'col', axis=0, tiled=True)  67.2 us
    psum x1, waiting for transfers between devices, shards(): weight_grad = lax.psum(local_grad, ('row', 'col'))  62.6 us
    scatter-add x2, other arithmetic, tile_product(): jnp.zeros((put_count, size_block, width), jnp.float32).at[put_ids]  56.8 us
    all_gather x1, waiting for transfers between devices, shards(): feature_tile = lax.all_gather(features, 'row', axis=0, tiled=True)  55 us
    dot_general x2, matrix products, tile_product(): products = jnp.einsum(form, values, chosen, precision=lax.Precision.HIGHEST)  53.9 us
    dot_general x2, local copies, waits for them, and re-layouts, tile_product(): products = jnp.einsum(form, values, chosen, precision=lax.Precision.HIGHEST)  25.1 us
  transfers between devices with their start and end apart: 5, of which 5 were waited for; matrix products, arithmetic and copies ran while one was open for 16% of the time, Pallas kernels for 0%

commit v1 on v0

v1 whole, which is shorter than its diff:
```python
import math
import jax
import jax.numpy as jnp
from jax import lax
from jax.experimental import pallas as pl
from jax.experimental.pallas import tpu as pltpu
from jax.sharding import PartitionSpec as P

F32 = jnp.float32
BF16 = jnp.bfloat16
MESH = pl.DeviceIdType.MESH
HA = 0
HB = 2
N_SEM = 192
FAR = 1 << 20


def split(value):
    high = value.astype(BF16)
    return high, (value - high.astype(F32)).astype(BF16)


def dot(a, b):
    return jnp.dot(a, b, preferred_element_type=F32)


def dot3(ah, al, bh, bl):
    return dot(ah, bh) + dot(al, bh) + dot(ah, bl)


def sort_tables(ids, table, base, scratch, other, sources):
    count = ids.shape[-1]
    scratch[...] = jnp.full(scratch.shape, FAR, jnp.int32)
    scratch[0:1, 0:count] = ids
    scratch[1:2, 0:count] = other
    lane_ids = jnp.broadcast_to(scratch[0:1, :], (128, 128))
    lane_other = jnp.broadcast_to(scratch[1:2, :], (128, 128))
    sub_ids, sub_other = lane_ids.T, lane_other.T
    lane = lax.broadcasted_iota(jnp.int32, (128, 128), 1)
    sub = lax.broadcasted_iota(jnp.int32, (128, 128), 0)

    def total(mask, value, axis):
        return jnp.sum(jnp.where(mask, value, 0), axis=axis, keepdims=True)

    rank = total((lane_ids < sub_ids) | ((lane_ids == sub_ids) & (lane < sub)), 1, 1)
    below = total(lane_ids < sub_ids, 1, 1)
    here = (jnp.broadcast_to(rank, (128, 128)) == lane) & (sub < count)
    order = total(here, sub, 0)
    source = total(here, sub_other, 0)
    starts = total(here, jnp.broadcast_to(below, (128, 128)), 0)
    upto = total(sub_ids <= lane, 1, 0)
    same = total(sub_ids == lane, 1, 0)
    table[base : base + 1, :] = jnp.clip(order, 0, count - 1)
    table[base + 1 : base + 2, :] = jnp.clip(source, 0, sources - 1)
    table[base + 2 : base + 3, :] = jnp.where(starts == lane[0:1, :], 1, 0)
    table[base + 3 : base + 4, :] = jnp.clip(upto - 1, 0, count - 1)
    table[base + 4 : base + 5, :] = jnp.where(same > 0, 1, 0)


class Links:
    def __init__(self, send_sem, recv_sem):
        self.send_sem, self.recv_sem, self.used, self.open = send_sem, recv_sem, 0, []

    def send(self, src, dst, device):
        i = self.used
        self.used += 1
        assert i < N_SEM
        copy = pltpu.make_async_remote_copy(
            src_ref=src, dst_ref=dst, send_sem=self.send_sem.at[i], recv_sem=self.recv_sem.at[i],
            device_id=device, device_id_type=MESH)
        copy.start()
        self.open.append(copy)
        return copy

    def flush(self):
        for copy in self.open:
            copy.wait_send()
        self.open = []


class GatherRing:
    def __init__(self, links, view, pos, plus, minus):
        self.links, self.view, self.pos, self.plus, self.minus = links, view, pos, plus, minus

    def start(self):
        view, q, send = self.view, self.pos, self.links.send
        a, b = view(q, HA, 2), view(q, HB, 2)
        self.c1 = send(a, a, self.plus)
        self.c2 = send(b, b, self.minus)
        self.c3 = send(b, b, self.plus)
        self.c4 = send(a, a, self.minus)

    def relay(self):
        view, q, send = self.view, self.pos, self.links.send
        left, right = lax.rem(q + 3, 4), lax.rem(q + 1, 4)
        self.c1.wait_recv()
        a = view(left, HA, 2)
        self.r1 = send(a, a, self.plus)
        self.c2.wait_recv()
        b = view(right, HB, 2)
        self.r2 = send(b, b, self.minus)

    def finish(self, arrived=None):
        view, q = self.view, self.pos
        self.c3.wait_recv()
        if arrived:
            arrived(view(lax.rem(q + 3, 4), HA, 4))
        self.c4.wait_recv()
        if arrived:
            arrived(view(lax.rem(q + 1, 4), HA, 4))
        self.r1.wait_recv()
        self.r2.wait_recv()
        if arrived:
            arrived(view(lax.rem(q + 2, 4), HA, 4))


class SumRing:
    def __init__(self, links, view, near, far, pos, plus, minus):
        self.links, self.view, self.near, self.far = links, view, near, far
        self.pos, self.plus, self.minus = pos, plus, minus

    def start(self):
        view, q, send = self.view, self.pos, self.links.send
        left, right, across = lax.rem(q + 3, 4), lax.rem(q + 1, 4), lax.rem(q + 2, 4)
        self.o1 = send(view(across, HA, 2), self.near.at[0], self.plus)
        self.o2 = send(view(across, HB, 2), self.near.at[1], self.minus)
        self.n1 = send(view(right, HB, 2), self.far.at[0, 2:4], self.plus)
        self.n2 = send(view(left, HA, 2), self.far.at[1, 0:2], self.minus)

    def relay(self):
        view, q, send = self.view, self.pos, self.links.send
        left, right = lax.rem(q + 3, 4), lax.rem(q + 1, 4)
        self.o1.wait_recv()
        part = view(right, HA, 2)
        part[...] += self.near[0]
        self.m1 = send(part, self.far.at[0, 0:2], self.plus)
        self.o2.wait_recv()
        part = view(left, HB, 2)
        part[...] += self.near[1]
        self.m2 = send(part, self.far.at[1, 2:4], self.minus)

    def finish(self):
        self.n1.wait_recv()
        self.n2.wait_recv()
        self.m1.wait_recv()
        self.m2.wait_recv()
        part = self.view(self.pos, HA, 4)
        part[...] += self.far[0] + self.far[1]
        return part


def kernel(total_nodes, feats, weight, cot, rows_in, cols_in, blocks, hidden_out, wgrad_out, fgrad_out,
           X, XX, A, AT, PS, OUT, BK, DR, CN, CF, CX, RN, RF, RX, W_ref, C_ref, AG, DP, HID, G, WH, WR, WS, WO,
           WP, IDS, TAB, TABS, send_sem, recv_sem, load_sem):
    row, col = lax.axis_index("row"), lax.axis_index("col")
    y, x_lo, core = row // 4, lax.rem(row // 2, 2), lax.rem(row, 2)
    z, x_hi = col // 2, lax.rem(col, 2)
    chip = row // 2

    def at_row(yy, xx, cc):
        return (yy * 4 + xx * 2 + cc, col)

    def at_col(zz, xx):
        return (row, zz * 2 + xx)

    y_plus, y_minus = at_row(lax.rem(y + 1, 4), x_lo, core), at_row(lax.rem(y + 3, 4), x_lo, core)
    z_plus, z_minus = at_col(lax.rem(z + 1, 4), x_hi), at_col(lax.rem(z + 3, 4), x_hi)
    x_near, twin, x_far = at_row(y, 1 - x_lo, core), at_row(y, x_lo, 1 - core), at_col(z, 1 - x_hi)
    col_peers = [(row, lax.rem(col + j, 8)) for j in range(1, 8)]
    row_peers = [(lax.rem(chip + j, 8) * 2 + core, col) for j in range(1, 8)]

    loads = []

    def load(src, dst):
        copy = pltpu.make_async_copy(src, dst, load_sem.at[len(loads)])
        copy.start()
        loads.append(copy)
        return copy

    lanes = [pl.ds(f * 128, 128) for f in range(2)]
    mine_x = [X.at[f, pl.ds(row * 4, 4)] for f in range(2)]
    get_x = [load(feats.at[:, :, lanes[f]], mine_x[f]) for f in range(2)]
    get_a = load(blocks, PS)
    get_w = load(weight, W_ref)
    get_c = load(cot, C_ref)

    barrier = pltpu.get_barrier_semaphore()
    peers = col_peers + row_peers + [twin]
    for peer in peers:
        pl.semaphore_signal(barrier, inc=1, device_id=peer, device_id_type=MESH)
    pl.semaphore_wait(barrier, len(peers))

    links = Links(send_sem, recv_sem)
    send = links.send

    def x_view(f, xx):
        return lambda q, half, n: X.at[f, pl.ds((q * 4 + xx * 2 + core) * 4 + half, n)]

    own = [GatherRing(links, x_view(f, x_lo), y, y_plus, y_minus) for f in range(2)]
    other = [GatherRing(links, x_view(f, 1 - x_lo), y, y_plus, y_minus) for f in range(2)]
    xs, twins = [None, None], [[], []]

    def to_twin(f):
        return lambda piece: twins[f].append(send(piece, piece, twin))

    get_x[0].wait()
    own[0].start()
    xs[0] = send(mine_x[0], mine_x[0], x_near)
    get_x[1].wait()
    xs[1] = send(mine_x[1], mine_x[1], x_near)
    to_twin(0)(mine_x[0])
    to_twin(1)(mine_x[1])

    sort_tables(rows_in[...], TAB, 0, IDS.at[0], cols_in[...], 64)
    sort_tables(cols_in[...], TAB, 8, IDS.at[1], rows_in[...], 32)
    get_tab = load(TAB, TABS)
    get_tab.wait()
    get_a.wait()

    def prepare(k, carry):
        value = PS[k]
        high, low = split(value)
        A[k, :, 0:128] = high
        A[k, :, 128:256] = low
        high, low = split(value.T)
        AT[k, :, 0:128] = high
        AT[k, :, 128:256] = low
        return carry

    lax.fori_loop(0, 32, prepare, 0)
    xs[0].wait_recv()
    other[0].start()
    to_twin(0)(x_view(0, 1 - x_lo)(y, HA, 4))
    lax.fori_loop(32, 64, prepare, 0)
    own[0].relay()
    other[0].relay()
    own[1].start()
    xs[1].wait_recv()
    other[1].start()
    to_twin(1)(x_view(1, 1 - x_lo)(y, HA, 4))
    lax.fori_loop(64, 96, prepare, 0)
    get_w.wait()
    high, low = split(W_ref[...])
    WP[0], WP[1] = high, low
    high, low = split(W_ref[...].T)
    WP[2], WP[3] = high, low
    get_c.wait()

    def to_pairs(source, f, count):
        def step(k, carry):
            high, low = split(source[f, k])
            XX[k, :, 0:128] = high
            XX[k, :, 128:256] = low
            return carry

        lax.fori_loop(0, count, step, 0, unroll=2)

    def tile_product(left, base):
        def step(p, total):
            lhs = left[TABS[base, p]]
            pair = XX[TABS[base + 1, p]]
            result = dot(lhs, jnp.concatenate([pair, pair], axis=0))
            term = result[:, 0:128] + result[:, 128:256]
            total = jnp.where(TABS[base + 2, p] == 1, term, total + term)
            PS[p] = total
            return total

        lax.fori_loop(0, PS.shape[0], step, jnp.zeros((128, 128), F32), unroll=4)

    def collect(dst, f, base, start, count, place):
        def step(r, carry):
            t = place(r)
            dst[f, t] = jnp.where(TABS[base + 4, t] == 1, PS[TABS[base + 3, t]], 0.0)
            return carry

        lax.fori_loop(start, start + count, step, 0, unroll=2)

    def same(r):
        return r

    def col_view(f, xx):
        return lambda q, half, n: OUT.at[f, pl.ds((q * 2 + xx) * 4 + half, n)]

    col_far = [SumRing(links, col_view(f, 1 - x_hi), CN.at[f, 0], CF.at[f, 0], z, z_plus, z_minus) for f in range(2)]
    col_own = [SumRing(links, col_view(f, x_hi), CN.at[f, 1], CF.at[f, 1], z, z_plus, z_minus) for f in range(2)]

    def finish_gather(f):
        own[f].finish(to_twin(f))
        other[f].finish(to_twin(f))
        for copy in twins[f]:
            copy.wait_recv()

    def forward(f):
        to_pairs(X, f, X.shape[1])
        tile_product(A, 0)
        collect(OUT, f, 0, 0, OUT.shape[1], same)
        col_far[f].start()
        col_own[f].start()

    finish_gather(0)
    forward(0)
    own[1].relay()
    other[1].relay()
    col_far[0].relay()
    col_own[0].relay()
    finish_gather(1)
    forward(1)
    sums = [None, None]
    sums[0] = send(col_far[0].finish(), CX.at[0], x_far)
    col_far[1].relay()
    col_own[1].relay()
    col_own[0].finish()
    sums[1] = send(col_far[1].finish(), CX.at[1], x_far)
    col_own[1].finish()
    for f in range(2):
        sums[f].wait_recv()

    def middle(i, carry):
        agg0 = OUT[0, col * 4 + i] + CX[0, i]
        agg1 = OUT[1, col * 4 + i] + CX[1, i]
        agg = jnp.concatenate([agg0, agg1], axis=1)
        ah, al = split(agg)
        pre = dot3(ah, al, WP[0], WP[1])
        sig = 1.0 / (1.0 + jnp.exp(-pre))
        HID[i] = pre * sig
        dpre = C_ref[i] * sig * (1.0 + pre * (1.0 - sig))
        dh, dl = split(dpre)
        back = dot3(dh, dl, WP[2], WP[3])
        BK[0, col * 4 + i] = back[:, 0:128]
        BK[1, col * 4 + i] = back[:, 128:256]
        AG[i] = agg
        DP[i] = dpre
        return carry

    lax.fori_loop(0, 4, middle, 0)

    def b_view(f, xx):
        return lambda q, half, n: BK.at[f, pl.ds((q * 2 + xx) * 4 + half, n)]

    own = [GatherRing(links, b_view(f, x_hi), z, z_plus, z_minus) for f in range(2)]
    other = [GatherRing(links, b_view(f, 1 - x_hi), z, z_plus, z_minus) for f in range(2)]
    mine_b = [BK.at[f, pl.ds(col * 4, 4)] for f in range(2)]
    own[0].start()
    xs = [send(mine_b[f], mine_b[f], x_far) for f in range(2)]
    put_h = load(HID, hidden_out)

    def term(i, total):
        th, tl = split(AG[i].T)
        dh, dl = split(DP[i])
        return total + dot3(th, tl, dh, dl)

    G[...] = lax.fori_loop(0, 4, term, jnp.zeros(G.shape, F32)) / jnp.float32(math.sqrt(total_nodes))
    half_of = lambda c: pl.ds(pl.multiple_of(c * 128, 128), 128)
    w1 = send(G.at[half_of(1 - core)], WH, twin)

    xs[0].wait_recv()
    other[0].start()
    w1.wait_recv()
    WH[...] += G[half_of(core), :]
    slot = lambda m: pl.ds(pl.multiple_of(m * 16, 16), 16)
    w2 = [send(WH.at[slot(peer[1])], WR.at[col], peer) for peer in col_peers]
    WR[col] = WH[slot(col), :]
    own[0].relay()
    other[0].relay()
    own[1].start()
    xs[1].wait_recv()
    other[1].start()
    for copy in w2:
        copy.wait_recv()

    def add_all(parts):
        total = parts[0]
        for m in range(1, 8):
            total = total + parts[m]
        return total

    WS[chip] = add_all(WR)
    w3 = [send(WS.at[chip], WS.at[chip], peer) for peer in row_peers]

    def r_view(f, xx):
        return lambda q, half, n: X.at[f, pl.ds((q * 4 + xx * 2 + core) * 4 + half, n)]

    row_far = [SumRing(links, r_view(f, 1 - x_lo), RN.at[f, 0], RF.at[f, 0], y, y_plus, y_minus) for f in range(2)]
    row_own = [SumRing(links, r_view(f, x_lo), RN.at[f, 1], RF.at[f, 1], y, y_plus, y_minus) for f in range(2)]

    def finish_back(f):
        own[f].finish()
        other[f].finish()

    links.flush()

    def backward(f):
        to_pairs(BK, f, BK.shape[1])
        tile_product(AT, 8)

        def part(c):
            return lambda r: (r // 4) * 8 + c * 4 + lax.rem(r, 4)

        collect(X, f, 8, 0, 32, part(1 - core))
        moves = []
        for m in range(8):
            b = m * 8 + (1 - core) * 4
            moves.append(send(X.at[f, pl.ds(b, 4)], DR.at[f, pl.ds(m * 4, 4)], twin))
        collect(X, f, 8, 0, 32, part(core))
        return moves

    def join(f, moves):
        for copy in moves:
            copy.wait_recv()

        def step(r, carry):
            t = (r // 4) * 8 + core * 4 + lax.rem(r, 4)
            X[f, t] += DR[f, r]
            return carry

        lax.fori_loop(0, 32, step, 0, unroll=2)
        row_far[f].start()
        row_own[f].start()

    finish_back(0)
    moves = backward(0)
    own[1].relay()
    other[1].relay()
    join(0, moves)
    for copy in w3:
        copy.wait_recv()
    mine_w = WO.at[pl.ds(pl.multiple_of(core * 128 + col * 16, 16), 16)]
    mine_w[...] = add_all(WS)
    w4 = [send(mine_w, mine_w, peer) for peer in col_peers]
    row_far[0].relay()
    row_own[0].relay()
    finish_back(1)
    moves = backward(1)
    for copy in w4:
        copy.wait_recv()
    w5 = send(WO.at[half_of(core)], WO.at[half_of(core)], twin)
    sums[0] = send(row_far[0].finish(), RX.at[0], x_near)
    join(1, moves)
    row_own[0].finish()
    row_far[1].relay()
    row_own[1].relay()
    w5.wait_recv()
    put_w = load(WO, wgrad_out)
    sums[1] = send(row_far[1].finish(), RX.at[1], x_near)
    sums[0].wait_recv()
    mine_x[0][...] += RX[0]
    put_0 = load(mine_x[0], fgrad_out.at[:, :, lanes[0]])
    row_own[1].finish()
    sums[1].wait_recv()
    mine_x[1][...] += RX[1]
    put_1 = load(mine_x[1], fgrad_out.at[:, :, lanes[1]])
    links.flush()
    for copy in (put_h, put_w, put_0, put_1):
        copy.wait()


def shards(features, weight_matrix, cotangent, block_rows, block_cols, blocks):
    assert lax.axis_size("row") == 16 and lax.axis_size("col") == 8
    count = blocks.shape[2]
    rows_dev, width = features.shape
    assert (rows_dev, width) == (512, 256) and blocks.shape[3] == 128 and count <= 128
    total_nodes = rows_dev * 128
    any_ = pl.BlockSpec(memory_space=pl.ANY)
    vmem = pl.BlockSpec(memory_space=pltpu.VMEM)
    out = [
        jax.ShapeDtypeStruct((4, 128, 256), F32),
        jax.ShapeDtypeStruct((256, 256), F32),
        jax.ShapeDtypeStruct((4, 128, 256), F32),
    ]
    scratch = [
        pltpu.VMEM((2, 64, 128, 128), F32),
        pltpu.VMEM((64, 128, 256), BF16),
        pltpu.VMEM((count, 128, 256), BF16),
        pltpu.VMEM((count, 128, 256), BF16),
        pltpu.VMEM((count, 128, 128), F32),
        pltpu.VMEM((2, 32, 128, 128), F32),
        pltpu.VMEM((2, 32, 128, 128), F32),
        pltpu.VMEM((2, 32, 128, 128), F32),
        pltpu.VMEM((2, 2, 2, 2, 128, 128), F32),
        pltpu.VMEM((2, 2, 2, 4, 128, 128), F32),
        pltpu.VMEM((2, 4, 128, 128), F32),
        pltpu.VMEM((2, 2, 2, 2, 128, 128), F32),
        pltpu.VMEM((2, 2, 2, 4, 128, 128), F32),
        pltpu.VMEM((2, 4, 128, 128), F32),
        pltpu.VMEM((256, 256), F32),
        pltpu.VMEM((4, 128, 256), F32),
        pltpu.VMEM((4, 128, 256), F32),
        pltpu.VMEM((4, 128, 256), F32),
        pltpu.VMEM((4, 128, 256), F32),
        pltpu.VMEM((256, 256), F32),
        pltpu.VMEM((128, 256), F32),
        pltpu.VMEM((8, 16, 256), F32),
        pltpu.VMEM((8, 16, 256), F32),
        pltpu.VMEM((256, 256), F32),
        pltpu.VMEM((4, 256, 256), BF16),
        pltpu.VMEM((2, 8, 128), jnp.int32),
        pltpu.VMEM((16, 128), jnp.int32),
        pltpu.SMEM((16, 128), jnp.int32),
        pltpu.SemaphoreType.DMA((N_SEM,)),
        pltpu.SemaphoreType.DMA((N_SEM,)),
        pltpu.SemaphoreType.DMA((16,)),
    ]
    hidden, weight_grad, feature_grad = pl.pallas_call(
        lambda *refs: kernel(total_nodes, *refs),
        out_shape=out,
        in_specs=[any_, any_, any_, vmem, vmem, any_],
        out_specs=[any_] * 3,
        scratch_shapes=scratch,
        compiler_params=pltpu.CompilerParams(
            collective_id=0, has_side_effects=True, vmem_limit_bytes=63 * 1024 * 1024
        ),
        name="graph_layer",
    )(
        features.reshape(4, 128, width),
        weight_matrix,
        cotangent.reshape(4, 128, width),
        block_rows[0],
        block_cols[0],
        blocks[0, 0],
    )
    return hidden.reshape(rows_dev, width), weight_grad, feature_grad.reshape(rows_dev, width)


def solution(mesh):
    in_specs = (
        P(("col", "row"), None),
        P(),
        P(("row", "col"), None),
        P("row", "col", None),
        P("row", "col", None),
        P("row", "col", None, None, None),
    )
    out_specs = (P(("row", "col"), None), P(), P(("col", "row"), None))
    return jax.shard_map(shards, mesh=mesh, in_specs=in_specs, out_specs=out_specs, check_vma=False)
```

time: 560 us -> 176 us (0.31)
  waiting for transfers between devices: 370 us -> 0 us
  Pallas kernels: 0 us -> 169 us
  matrix products: 60.7 us -> 0 us
  other arithmetic: 58.1 us -> 0 us
  local copies, waits for them, and re-layouts: 56.4 us -> 5.4 us
  between operations: 13.8 us -> 0.64 us
    reduce_scatter x2 -> x0, waiting for transfers between devices: 184 us -> none  [the longest x1 97.9 us: shards(): lax.psum_scatter(grad_part, 'row', scatter_dimension=0, tiled=True)]
    pallas_call x0 -> x1, Pallas kernels: none -> 169 us  [shards(): pl.pallas_call(lambda *refs: kernel(total_nodes, *refs), out_shape=out, i...]
    all_gather x2 -> x0, waiting for transfers between devices: 122 us -> none  [the longest x1 67.2 us: shards(): back_rows = lax.all_gather(back_own, 'col', axis=0, tiled=True)]
    psum x1 -> x0, waiting for transfers between devices: 62.6 us -> none  [shards(): weight_grad = lax.psum(local_grad, ('row', 'col'))]
    dot_general x5 -> x0, matrix products: 60.7 us -> none  [the longest x2 53.9 us: tile_product(): products = jnp.einsum(form, values, chosen, precision=lax.Precision.HIGHEST)]
    scatter-add x2 -> x0, other arithmetic: 56.8 us -> none  [tile_product(): jnp.zeros((put_count, size_block, width), jnp.float32).at[put_ids]]
    dot_general x2 -> x0, local copies, waits for them, and re-layouts: 25.1 us -> none  [tile_product(): products = jnp.einsum(form, values, chosen, precision=lax.Precision.HIGHEST)]
    gather x2 -> x0, local copies, waits for them, and re-layouts: 22.9 us -> none  [tile_product(): chosen = source.reshape(-1, size_block, width)[take_ids]]
  transfers between devices with their start and end apart: 5 -> 0, of which waited for: 5 -> 0; matrix products, arithmetic and copies ran while one was open for 16% -> 0% of each run, Pallas kernels for 0% -> 0%
where the time goes in v1:
time: 176 us; the launch traced here: 175 us
  Pallas kernels  169 us (96%)
  local copies, waits for them, and re-layouts  5.4 us (3%)
    pallas_call x1, Pallas kernels, shards(): pl.pallas_call(lambda *refs: kernel(total_nodes, *refs), out_shape=out, i...  169 us
    unnamed x3, local copies, waits for them, and re-layouts  5.4 us

profile of v1, /device:TPU:0, one launch (start us, length us, event | category | flops | bytes accessed | tf_op | source)
XLA Modules:
  0.0 174.7 jit_solution(5461957548300790332)
XLA Ops:
  0.6 168.7 %graph_layer.1 = (f32[4,128,256]{2,1,0:T(8,128)}, f32[256,256]{1,0:T(8,128)}, f32[4,128,256]{2,1,0:T(8,128)}) custom-call(f32[4,128,256]{2,1,0:T(8,128)} %bitcast.8, f32[256,256]{1,0:T(8,128)} %refs_1_.1, f32[4,128,256]{2,1,0:T(8,128)} %bitcast.9, s32[1,96]{1,0:T(1,128)} %bitcast.12, s32[1,96]{1,0:T(1,128)} %bitcast.13, f32[96,128,128]{2,1,0:T(8,128)} %bitcast.7), custom_call_target="tpu_custom_call" | custom-call | tf_op jit(solution)/shard_map/graph_layer/pallas_call | solution.py:503
  169.3 1.9 %copy.12 = f32[512,256]{1,0:T(8,128)} copy(f32[512,256]{1,0:T(8,128)} %bitcast.11) | data formatting | bytes 1048576
  171.2 1.7 copy.13
  172.8 1.9 %copy.14 = f32[512,256]{1,0:T(8,128)} copy(f32[512,256]{1,0:T(8,128)} %bitcast.10) | data formatting | bytes 1048576

commit v2 on v1

--- a/solution.py
+++ b/solution.py
@@ -82,13 +82,19 @@
     def __init__(self, links, view, pos, plus, minus):
         self.links, self.view, self.pos, self.plus, self.minus = links, view, pos, plus, minus
 
-    def start(self):
+    def start(self, halves=(None, None)):
         view, q, send = self.view, self.pos, self.links.send
         a, b = view(q, HA, 2), view(q, HB, 2)
+        if halves[0]:
+            halves[0].wait_recv()
         self.c1 = send(a, a, self.plus)
+        if halves[0]:
+            self.c4 = send(a, a, self.minus)
+            halves[1].wait_recv()
         self.c2 = send(b, b, self.minus)
         self.c3 = send(b, b, self.plus)
-        self.c4 = send(a, a, self.minus)
+        if not halves[0]:
+            self.c4 = send(a, a, self.minus)
 
     def relay(self):
         view, q, send = self.view, self.pos, self.links.send
@@ -203,11 +209,14 @@
     def to_twin(f):
         return lambda piece: twins[f].append(send(piece, piece, twin))
 
+    def across(view, pos, device):
+        return [send(view(pos, half, 2), view(pos, half, 2), device) for half in (HA, HB)]
+
     get_x[0].wait()
+    xs[0] = across(x_view(0, x_lo), y, x_near)
     own[0].start()
-    xs[0] = send(mine_x[0], mine_x[0], x_near)
     get_x[1].wait()
-    xs[1] = send(mine_x[1], mine_x[1], x_near)
+    xs[1] = across(x_view(1, x_lo), y, x_near)
     to_twin(0)(mine_x[0])
     to_twin(1)(mine_x[1])
 
@@ -227,18 +236,17 @@
         AT[k, :, 128:256] = low
         return carry
 
-    lax.fori_loop(0, 32, prepare, 0)
-    xs[0].wait_recv()
-    other[0].start()
+    lax.fori_loop(0, 16, prepare, 0)
+    other[0].start(xs[0])
     to_twin(0)(x_view(0, 1 - x_lo)(y, HA, 4))
-    lax.fori_loop(32, 64, prepare, 0)
+    lax.fori_loop(16, 32, prepare, 0)
     own[0].relay()
+    lax.fori_loop(32, 48, prepare, 0)
     other[0].relay()
     own[1].start()
-    xs[1].wait_recv()
-    other[1].start()
+    other[1].start(xs[1])
     to_twin(1)(x_view(1, 1 - x_lo)(y, HA, 4))
-    lax.fori_loop(64, 96, prepare, 0)
+    lax.fori_loop(48, 96, prepare, 0)
     get_w.wait()
     high, low = split(W_ref[...])
     WP[0], WP[1] = high, low
@@ -295,25 +303,27 @@
         tile_product(A, 0)
         collect(OUT, f, 0, 0, OUT.shape[1], same)
         col_far[f].start()
-        col_own[f].start()
 
     finish_gather(0)
     forward(0)
     own[1].relay()
+    col_far[0].relay()
+    col_own[0].start()
     other[1].relay()
-    col_far[0].relay()
+    finish_gather(1)
+    sums = [send(col_far[0].finish(), CX.at[0], x_far)]
     col_own[0].relay()
-    finish_gather(1)
     forward(1)
-    sums = [None, None]
-    sums[0] = send(col_far[0].finish(), CX.at[0], x_far)
+    col_own[0].finish()
     col_far[1].relay()
+    col_own[1].start()
+    sums.append(send(col_far[1].finish(), CX.at[1], x_far))
     col_own[1].relay()
-    col_own[0].finish()
-    sums[1] = send(col_far[1].finish(), CX.at[1], x_far)
     col_own[1].finish()
     for f in range(2):
         sums[f].wait_recv()
+
+    early, links.open = links.open, []
 
     def middle(i, carry):
         agg0 = OUT[0, col * 4 + i] + CX[0, i]
@@ -339,9 +349,9 @@
 
     own = [GatherRing(links, b_view(f, x_hi), z, z_plus, z_minus) for f in range(2)]
     other = [GatherRing(links, b_view(f, 1 - x_hi), z, z_plus, z_minus) for f in range(2)]
-    mine_b = [BK.at[f, pl.ds(col * 4, 4)] for f in range(2)]
+    xs = [across(b_view(0, x_hi), z, x_far)]
     own[0].start()
-    xs = [send(mine_b[f], mine_b[f], x_far) for f in range(2)]
+    xs.append(across(b_view(1, x_hi), z, x_far))
     put_h = load(HID, hidden_out)
 
     def term(i, total):
@@ -353,8 +363,7 @@
     half_of = lambda c: pl.ds(pl.multiple_of(c * 128, 128), 128)
     w1 = send(G.at[half_of(1 - core)], WH, twin)
 
-    xs[0].wait_recv()
-    other[0].start()
+    other[0].start(xs[0])
     w1.wait_recv()
     WH[...] += G[half_of(core), :]
     slot = lambda m: pl.ds(pl.multiple_of(m * 16, 16), 16)
@@ -363,8 +372,7 @@
     own[0].relay()
     other[0].relay()
     own[1].start()
-    xs[1].wait_recv()
-    other[1].start()
+    other[1].start(xs[1])
     for copy in w2:
         copy.wait_recv()
 
@@ -377,80 +385,101 @@
     WS[chip] = add_all(WR)
     w3 = [send(WS.at[chip], WS.at[chip], peer) for peer in row_peers]
 
-    def r_view(f, xx):
-        return lambda q, half, n: X.at[f, pl.ds((q * 4 + xx * 2 + core) * 4 + half, n)]
-
-    row_far = [SumRing(links, r_view(f, 1 - x_lo), RN.at[f, 0], RF.at[f, 0], y, y_plus, y_minus) for f in range(2)]
-    row_own = [SumRing(links, r_view(f, x_lo), RN.at[f, 1], RF.at[f, 1], y, y_plus, y_minus) for f in range(2)]
+    def r_view(f, xx, cc):
+        return lambda q, half, n: X.at[f, pl.ds((q * 4 + xx * 2 + cc) * 4 + half, n)]
+
+    def part(xx, cc):
+        return lambda r: ((r // 4) * 4 + xx * 2 + cc) * 4 + lax.rem(r, 4)
+
+    row_far = [SumRing(links, r_view(f, 1 - x_lo, core), RN.at[f, 0], RF.at[f, 0], y, y_plus, y_minus) for f in range(2)]
+    row_own = [SumRing(links, r_view(f, x_lo, core), RN.at[f, 1], RF.at[f, 1], y, y_plus, y_minus) for f in range(2)]
 
     def finish_back(f):
         own[f].finish()
         other[f].finish()
 
-    links.flush()
+    for copy in early:
+        copy.wait_send()
 
     def backward(f):
         to_pairs(BK, f, BK.shape[1])
         tile_product(AT, 8)
 
-        def part(c):
-            return lambda r: (r // 4) * 8 + c * 4 + lax.rem(r, 4)
-
-        collect(X, f, 8, 0, 32, part(1 - core))
         moves = []
-        for m in range(8):
-            b = m * 8 + (1 - core) * 4
-            moves.append(send(X.at[f, pl.ds(b, 4)], DR.at[f, pl.ds(m * 4, 4)], twin))
-        collect(X, f, 8, 0, 32, part(core))
+        for k, xx in enumerate((1 - x_lo, x_lo)):
+            collect(X, f, 8, 0, 16, part(xx, 1 - core))
+            for m in range(4):
+                moves.append(send(r_view(f, xx, 1 - core)(m, HA, 4), DR.at[f, pl.ds(k * 16 + m * 4, 4)], twin))
+        for xx in (1 - x_lo, x_lo):
+            collect(X, f, 8, 0, 16, part(xx, core))
         return moves
 
-    def join(f, moves):
-        for copy in moves:
+    def join(f, moves, k):
+        for copy in moves[k * 4 : k * 4 + 4]:
             copy.wait_recv()
+        place = part(x_lo if k else 1 - x_lo, core)
 
         def step(r, carry):
-            t = (r // 4) * 8 + core * 4 + lax.rem(r, 4)
-            X[f, t] += DR[f, r]
+            X[f, place(r)] += DR[f, k * 16 + r]
             return carry
 
-        lax.fori_loop(0, 32, step, 0, unroll=2)
-        row_far[f].start()
-        row_own[f].start()
+        lax.fori_loop(0, 16, step, 0, unroll=2)
 
     finish_back(0)
     moves = backward(0)
     own[1].relay()
+    join(0, moves, 0)
+    row_far[0].start()
+    join(0, moves, 1)
     other[1].relay()
-    join(0, moves)
     for copy in w3:
         copy.wait_recv()
     mine_w = WO.at[pl.ds(pl.multiple_of(core * 128 + col * 16, 16), 16)]
     mine_w[...] = add_all(WS)
     w4 = [send(mine_w, mine_w, peer) for peer in col_peers]
     row_far[0].relay()
-    row_own[0].relay()
+    row_own[0].start()
     finish_back(1)
     moves = backward(1)
+    row_own[0].relay()
+    sums = [send(row_far[0].finish(), RX.at[0], x_near)]
+    join(1, moves, 0)
+    row_far[1].start()
+    join(1, moves, 1)
     for copy in w4:
         copy.wait_recv()
     w5 = send(WO.at[half_of(core)], WO.at[half_of(core)], twin)
-    sums[0] = send(row_far[0].finish(), RX.at[0], x_near)
-    join(1, moves)
     row_own[0].finish()
     row_far[1].relay()
-    row_own[1].relay()
+    row_own[1].start()
     w5.wait_recv()
     put_w = load(WO, wgrad_out)
-    sums[1] = send(row_far[1].finish(), RX.at[1], x_near)
     sums[0].wait_recv()
     mine_x[0][...] += RX[0]
     put_0 = load(mine_x[0], fgrad_out.at[:, :, lanes[0]])
+    sums.append(send(row_far[1].finish(), RX.at[1], x_near))
+    row_own[1].relay()
     row_own[1].finish()
     sums[1].wait_recv()
     mine_x[1][...] += RX[1]
     put_1 = load(mine_x[1], fgrad_out.at[:, :, lanes[1]])
     links.flush()
     for copy in (put_h, put_w, put_0, put_1):
+        copy.wait()
+
+
+def hand_over(*refs):
+    count = len(refs) // 3
+    sources, results, held = refs[:count], refs[count : 2 * count], refs[2 * count : 3 * count]
+    in_sem, out_sem = refs[3 * count :]
+    ins = [pltpu.make_async_copy(sources[i], held[i], in_sem.at[i]) for i in range(count)]
+    outs = [pltpu.make_async_copy(held[i], results[i], out_sem.at[i]) for i in range(count)]
+    for copy in ins:
+        copy.start()
+    for i in range(count):
+        ins[i].wait()
+        outs[i].start()
+    for copy in outs:
         copy.wait()
 
 
@@ -500,7 +529,7 @@
         pltpu.SemaphoreType.DMA((N_SEM,)),
         pltpu.SemaphoreType.DMA((16,)),
     ]
-    hidden, weight_grad, feature_grad = pl.pallas_call(
+    made = pl.pallas_call(
         lambda *refs: kernel(total_nodes, *refs),
         out_shape=out,
         in_specs=[any_, any_, any_, vmem, vmem, any_],
@@ -518,6 +547,14 @@
         block_cols[0],
         blocks[0, 0],
     )
+    hidden, weight_grad, feature_grad = pl.pallas_call(
+        hand_over,
+        out_shape=out,
+        in_specs=[any_] * 3,
+        out_specs=[any_] * 3,
+        scratch_shapes=[pltpu.VMEM(a.shape, F32) for a in out] + [pltpu.SemaphoreType.DMA((3,))] * 2,
+        name="hand_over",
+    )(*made)
     return hidden.reshape(rows_dev, width), weight_grad, feature_grad.reshape(rows_dev, width)
 
 

time: 176 us -> 151 us (0.86)
  Pallas kernels: 169 us -> 150 us
  local copies, waits for them, and re-layouts: 5.4 us -> 0 us
    pallas_call x1, Pallas kernels: 169 us -> 148 us  [shards(): pl.pallas_call(lambda *refs: kernel(total_nodes, *refs), out_shape=out, i...]
    unnamed x3 -> x0, local copies, waits for them, and re-layouts: 5.4 us -> none
    pallas_call x0 -> x1, Pallas kernels: none -> 2.15 us  [shards(): pl.pallas_call(hand_over, out_shape=out, in_specs=[any_] * 3, out_specs=[...]
where the time goes in v2:
time: 151 us
  Pallas kernels  150 us (99%)
    pallas_call x1, Pallas kernels, shards(): pl.pallas_call(lambda *refs: kernel(total_nodes, *refs), out_shape=out, i...  148 us

profile of v2, /device:TPU:0, one launch (start us, length us, event | category | flops | bytes accessed | tf_op | source)
XLA Modules:
  0.0 150.9 jit_solution(14025388539553101860)
XLA Ops:
  0.6 148.1 %graph_layer.1 = (f32[4,128,256]{2,1,0:T(8,128)}, f32[256,256]{1,0:T(8,128)}, f32[4,128,256]{2,1,0:T(8,128)}) custom-call(f32[4,128,256]{2,1,0:T(8,128)} %bitcast.8, f32[256,256]{1,0:T(8,128)} %refs_1_.1, f32[4,128,256]{2,1,0:T(8,128)} %bitcast.9, s32[1,96]{1,0:T(1,128)} %bitcast.10, s32[1,96]{1,0:T(1,128)} %bitcast.11, f32[96,128,128]{2,1,0:T(8,128)} %bitcast.7), custom_call_target="tpu_custom_call" | custom-call | tf_op jit(solution)/shard_map/graph_layer/pallas_call | solution.py:532
  148.8 2.1 %hand_over.1 = (f32[4,128,256]{2,1,0:T(8,128)}, f32[256,256]{1,0:T(8,128)}, f32[4,128,256]{2,1,0:T(8,128)}) custom-call(f32[4,128,256]{2,1,0:T(8,128)} %get-tuple-element.9.refs_0_, f32[256,256]{1,0:T(8,128)} %get-tuple-element.10.refs_1_, f32[4,128,256]{2,1,0:T(8,128)} %get-tuple-element.11.refs_2_), custom_call_target="tpu_custom_call" | custom-call | tf_op jit(solution)/shard_map/hand_over/pallas_call | solution.py:550

commit v3 on v2

--- a/solution.py
+++ b/solution.py
@@ -79,45 +79,54 @@
 
 
 class GatherRing:
-    def __init__(self, links, view, pos, plus, minus):
+    def __init__(self, links, view, pos, plus, minus, size, cross=None):
         self.links, self.view, self.pos, self.plus, self.minus = links, view, pos, plus, minus
-
-    def start(self, halves=(None, None)):
-        view, q, send = self.view, self.pos, self.links.send
-        a, b = view(q, HA, 2), view(q, HB, 2)
-        if halves[0]:
-            halves[0].wait_recv()
+        self.half, self.cross = size // 2, cross
+        self.left, self.right, self.across = lax.rem(pos + 3, 4), lax.rem(pos + 1, 4), lax.rem(pos + 2, 4)
+
+    def pieces(self, pos):
+        return self.view(pos, 0, self.half), self.view(pos, self.half, self.half)
+
+    def start(self):
+        send = self.links.send
+        a, b = self.pieces(self.pos)
         self.c1 = send(a, a, self.plus)
-        if halves[0]:
-            self.c4 = send(a, a, self.minus)
-            halves[1].wait_recv()
         self.c2 = send(b, b, self.minus)
         self.c3 = send(b, b, self.plus)
-        if not halves[0]:
-            self.c4 = send(a, a, self.minus)
+        self.c4 = send(a, a, self.minus)
 
     def relay(self):
-        view, q, send = self.view, self.pos, self.links.send
-        left, right = lax.rem(q + 3, 4), lax.rem(q + 1, 4)
+        send = self.links.send
         self.c1.wait_recv()
-        a = view(left, HA, 2)
+        a = self.pieces(self.left)[0]
         self.r1 = send(a, a, self.plus)
         self.c2.wait_recv()
-        b = view(right, HB, 2)
+        b = self.pieces(self.right)[1]
         self.r2 = send(b, b, self.minus)
-
-    def finish(self, arrived=None):
-        view, q = self.view, self.pos
+        if self.cross:
+            self.crossed = [send(b, b, self.cross)]
+
+    def cross_left(self):
         self.c3.wait_recv()
+        b = self.pieces(self.left)[1]
+        self.crossed.append(self.links.send(b, b, self.cross))
+
+    def cross_far(self):
+        self.r2.wait_recv()
+        b = self.pieces(self.across)[1]
+        self.crossed.append(self.links.send(b, b, self.cross))
+
+    def finish(self, arrived=None, crossed=()):
+        if not self.cross:
+            self.c3.wait_recv()
+            self.r2.wait_recv()
+        self.c4.wait_recv()
+        self.r1.wait_recv()
+        for copy in crossed:
+            copy.wait_recv()
         if arrived:
-            arrived(view(lax.rem(q + 3, 4), HA, 4))
-        self.c4.wait_recv()
-        if arrived:
-            arrived(view(lax.rem(q + 1, 4), HA, 4))
-        self.r1.wait_recv()
-        self.r2.wait_recv()
-        if arrived:
-            arrived(view(lax.rem(q + 2, 4), HA, 4))
+            for pos in (self.left, self.right, self.across):
+                arrived(self.view(pos, HA, 4))
 
 
 class SumRing:
@@ -202,8 +211,8 @@
     def x_view(f, xx):
         return lambda q, half, n: X.at[f, pl.ds((q * 4 + xx * 2 + core) * 4 + half, n)]
 
-    own = [GatherRing(links, x_view(f, x_lo), y, y_plus, y_minus) for f in range(2)]
-    other = [GatherRing(links, x_view(f, 1 - x_lo), y, y_plus, y_minus) for f in range(2)]
+    own = [GatherRing(links, x_view(f, x_lo), y, y_plus, y_minus, 4, x_near) for f in range(2)]
+    other = [GatherRing(links, x_view(f, 1 - x_lo), y, y_plus, y_minus, 2) for f in range(2)]
     xs, twins = [None, None], [[], []]
 
     def to_twin(f):
@@ -216,7 +225,6 @@
     xs[0] = across(x_view(0, x_lo), y, x_near)
     own[0].start()
     get_x[1].wait()
-    xs[1] = across(x_view(1, x_lo), y, x_near)
     to_twin(0)(mine_x[0])
     to_twin(1)(mine_x[1])
 
@@ -236,16 +244,18 @@
         AT[k, :, 128:256] = low
         return carry
 
+    own[0].relay()
+    xs[0][0].wait_recv()
+    other[0].start()
     lax.fori_loop(0, 16, prepare, 0)
-    other[0].start(xs[0])
+    own[0].cross_left()
+    xs[0][1].wait_recv()
     to_twin(0)(x_view(0, 1 - x_lo)(y, HA, 4))
-    lax.fori_loop(16, 32, prepare, 0)
-    own[0].relay()
-    lax.fori_loop(32, 48, prepare, 0)
+    lax.fori_loop(16, 48, prepare, 0)
     other[0].relay()
+    own[0].cross_far()
     own[1].start()
-    other[1].start(xs[1])
-    to_twin(1)(x_view(1, 1 - x_lo)(y, HA, 4))
+    xs[1] = across(x_view(1, x_lo), y, x_near)
     lax.fori_loop(48, 96, prepare, 0)
     get_w.wait()
     high, low = split(W_ref[...])
@@ -263,7 +273,7 @@
 
         lax.fori_loop(0, count, step, 0, unroll=2)
 
-    def tile_product(left, base):
+    def tile_product(left, base, between=None):
         def step(p, total):
             lhs = left[TABS[base, p]]
             pair = XX[TABS[base + 1, p]]
@@ -273,7 +283,11 @@
             PS[p] = total
             return total
 
-        lax.fori_loop(0, PS.shape[0], step, jnp.zeros((128, 128), F32), unroll=4)
+        middle = PS.shape[0] // 2
+        total = lax.fori_loop(0, middle, step, jnp.zeros((128, 128), F32), unroll=4)
+        if between:
+            between()
+        lax.fori_loop(middle, PS.shape[0], step, total, unroll=4)
 
     def collect(dst, f, base, start, count, place):
         def step(r, carry):
@@ -294,22 +308,30 @@
 
     def finish_gather(f):
         own[f].finish(to_twin(f))
-        other[f].finish(to_twin(f))
+        other[f].finish(to_twin(f), own[f].crossed)
         for copy in twins[f]:
             copy.wait_recv()
 
-    def forward(f):
+    def forward(f, between=None):
         to_pairs(X, f, X.shape[1])
-        tile_product(A, 0)
+        tile_product(A, 0, between)
         collect(OUT, f, 0, 0, OUT.shape[1], same)
         col_far[f].start()
 
+    def next_half():
+        own[1].relay()
+        xs[1][0].wait_recv()
+        other[1].start()
+
     finish_gather(0)
-    forward(0)
-    own[1].relay()
+    forward(0, next_half)
+    own[1].cross_left()
+    xs[1][1].wait_recv()
+    to_twin(1)(x_view(1, 1 - x_lo)(y, HA, 4))
+    other[1].relay()
+    own[1].cross_far()
     col_far[0].relay()
     col_own[0].start()
-    other[1].relay()
     finish_gather(1)
     sums = [send(col_far[0].finish(), CX.at[0], x_far)]
     col_own[0].relay()
@@ -347,11 +369,10 @@
     def b_view(f, xx):
         return lambda q, half, n: BK.at[f, pl.ds((q * 2 + xx) * 4 + half, n)]
 
-    own = [GatherRing(links, b_view(f, x_hi), z, z_plus, z_minus) for f in range(2)]
-    other = [GatherRing(links, b_view(f, 1 - x_hi), z, z_plus, z_minus) for f in range(2)]
+    own = [GatherRing(links, b_view(f, x_hi), z, z_plus, z_minus, 4, x_far) for f in range(2)]
+    other = [GatherRing(links, b_view(f, 1 - x_hi), z, z_plus, z_minus, 2) for f in range(2)]
     xs = [across(b_view(0, x_hi), z, x_far)]
     own[0].start()
-    xs.append(across(b_view(1, x_hi), z, x_far))
     put_h = load(HID, hidden_out)
 
     def term(i, total):
@@ -363,16 +384,19 @@
     half_of = lambda c: pl.ds(pl.multiple_of(c * 128, 128), 128)
     w1 = send(G.at[half_of(1 - core)], WH, twin)
 
-    other[0].start(xs[0])
+    own[0].relay()
+    xs[0][0].wait_recv()
+    other[0].start()
     w1.wait_recv()
     WH[...] += G[half_of(core), :]
     slot = lambda m: pl.ds(pl.multiple_of(m * 16, 16), 16)
     w2 = [send(WH.at[slot(peer[1])], WR.at[col], peer) for peer in col_peers]
     WR[col] = WH[slot(col), :]
-    own[0].relay()
+    own[0].cross_left()
     other[0].relay()
+    own[0].cross_far()
     own[1].start()
-    other[1].start(xs[1])
+    xs.append(across(b_view(1, x_hi), z, x_far))
     for copy in w2:
         copy.wait_recv()
 
@@ -396,14 +420,15 @@
 
     def finish_back(f):
         own[f].finish()
-        other[f].finish()
+        xs[f][1].wait_recv()
+        other[f].finish(None, own[f].crossed)
 
     for copy in early:
         copy.wait_send()
 
-    def backward(f):
+    def backward(f, between=None):
         to_pairs(BK, f, BK.shape[1])
-        tile_product(AT, 8)
+        tile_product(AT, 8, between)
 
         moves = []
         for k, xx in enumerate((1 - x_lo, x_lo)):
@@ -426,12 +451,13 @@
         lax.fori_loop(0, 16, step, 0, unroll=2)
 
     finish_back(0)
-    moves = backward(0)
-    own[1].relay()
+    moves = backward(0, next_half)
+    own[1].cross_left()
     join(0, moves, 0)
     row_far[0].start()
+    other[1].relay()
+    own[1].cross_far()
     join(0, moves, 1)
-    other[1].relay()
     for copy in w3:
         copy.wait_recv()
     mine_w = WO.at[pl.ds(pl.multiple_of(core * 128 + col * 16, 16), 16)]

time: 151 us -> 146 us (0.967)
  Pallas kernels: 150 us -> 145 us
    pallas_call x1, Pallas kernels: 148 us -> 143 us  [shards(): pl.pallas_call(lambda *refs: kernel(total_nodes, *refs), out_shape=out, i...]
where the time goes in v3:
time: 146 us
  Pallas kernels  145 us (99%)
    pallas_call x1, Pallas kernels, shards(): pl.pallas_call(lambda *refs: kernel(total_nodes, *refs), out_shape=out, i...  143 us

profile of v3, /device:TPU:0, one launch (start us, length us, event | category | flops | bytes accessed | tf_op | source)
XLA Modules:
  0.0 145.5 jit_solution(261125560982270026)
XLA Ops:
  0.6 142.7 %graph_layer.1 = (f32[4,128,256]{2,1,0:T(8,128)}, f32[256,256]{1,0:T(8,128)}, f32[4,128,256]{2,1,0:T(8,128)}) custom-call(f32[4,128,256]{2,1,0:T(8,128)} %bitcast.8, f32[256,256]{1,0:T(8,128)} %refs_1_.1, f32[4,128,256]{2,1,0:T(8,128)} %bitcast.9, s32[1,96]{1,0:T(1,128)} %bitcast.10, s32[1,96]{1,0:T(1,128)} %bitcast.11, f32[96,128,128]{2,1,0:T(8,128)} %bitcast.7), custom_call_target="tpu_custom_call" | custom-call | tf_op jit(solution)/shard_map/graph_layer/pallas_call | solution.py:558
  143.4 2.1 %hand_over.1 = (f32[4,128,256]{2,1,0:T(8,128)}, f32[256,256]{1,0:T(8,128)}, f32[4,128,256]{2,1,0:T(8,128)}) custom-call(f32[4,128,256]{2,1,0:T(8,128)} %get-tuple-element.9.refs_0_, f32[256,256]{1,0:T(8,128)} %get-tuple-element.10.refs_1_, f32[4,128,256]{2,1,0:T(8,128)} %get-tuple-element.11.refs_2_), custom_call_target="tpu_custom_call" | custom-call | tf_op jit(solution)/shard_map/hand_over/pallas_call | solution.py:576

commit v4 on v3

--- a/solution.py
+++ b/solution.py
@@ -247,16 +247,16 @@
     own[0].relay()
     xs[0][0].wait_recv()
     other[0].start()
-    lax.fori_loop(0, 16, prepare, 0)
+    lax.fori_loop(0, 16, prepare, 0, unroll=2)
     own[0].cross_left()
     xs[0][1].wait_recv()
     to_twin(0)(x_view(0, 1 - x_lo)(y, HA, 4))
-    lax.fori_loop(16, 48, prepare, 0)
+    lax.fori_loop(16, 48, prepare, 0, unroll=2)
     other[0].relay()
     own[0].cross_far()
     own[1].start()
     xs[1] = across(x_view(1, x_lo), y, x_near)
-    lax.fori_loop(48, 96, prepare, 0)
+    lax.fori_loop(48, 96, prepare, 0, unroll=2)
     get_w.wait()
     high, low = split(W_ref[...])
     WP[0], WP[1] = high, low
@@ -271,7 +271,7 @@
             XX[k, :, 128:256] = low
             return carry
 
-        lax.fori_loop(0, count, step, 0, unroll=2)
+        lax.fori_loop(0, count, step, 0, unroll=4)
 
     def tile_product(left, base, between=None):
         def step(p, total):
@@ -284,10 +284,10 @@
             return total
 
         middle = PS.shape[0] // 2
-        total = lax.fori_loop(0, middle, step, jnp.zeros((128, 128), F32), unroll=4)
+        total = lax.fori_loop(0, middle, step, jnp.zeros((128, 128), F32), unroll=16)
         if between:
             between()
-        lax.fori_loop(middle, PS.shape[0], step, total, unroll=4)
+        lax.fori_loop(middle, PS.shape[0], step, total, unroll=16)
 
     def collect(dst, f, base, start, count, place):
         def step(r, carry):
@@ -295,7 +295,7 @@
             dst[f, t] = jnp.where(TABS[base + 4, t] == 1, PS[TABS[base + 3, t]], 0.0)
             return carry
 
-        lax.fori_loop(start, start + count, step, 0, unroll=2)
+        lax.fori_loop(start, start + count, step, 0, unroll=4)
 
     def same(r):
         return r
@@ -448,7 +448,7 @@
             X[f, place(r)] += DR[f, k * 16 + r]
             return carry
 
-        lax.fori_loop(0, 16, step, 0, unroll=2)
+        lax.fori_loop(0, 16, step, 0, unroll=4)
 
     finish_back(0)
     moves = backward(0, next_half)

time: 146 us -> 137 us (0.938)
  Pallas kernels: 145 us -> 135 us
    pallas_call x1, Pallas kernels: 143 us -> 133 us  [shards(): pl.pallas_call(lambda *refs: kernel(total_nodes, *refs), out_shape=out, i...]
where the time goes in v4:
time: 137 us; the launch traced here: 136 us
  Pallas kernels  135 us (99%)
    pallas_call x1, Pallas kernels, shards(): pl.pallas_call(lambda *refs: kernel(total_nodes, *refs), out_shape=out, i...  133 us

profile of v4, /device:TPU:0, one launch (start us, length us, event | category | flops | bytes accessed | tf_op | source)
XLA Modules:
  0.0 135.5 jit_solution(6934433404957732489)
XLA Ops:
  0.6 132.7 %graph_layer.1 = (f32[4,128,256]{2,1,0:T(8,128)}, f32[256,256]{1,0:T(8,128)}, f32[4,128,256]{2,1,0:T(8,128)}) custom-call(f32[4,128,256]{2,1,0:T(8,128)} %bitcast.8, f32[256,256]{1,0:T(8,128)} %refs_1_.1, f32[4,128,256]{2,1,0:T(8,128)} %bitcast.9, s32[1,96]{1,0:T(1,128)} %bitcast.10, s32[1,96]{1,0:T(1,128)} %bitcast.11, f32[96,128,128]{2,1,0:T(8,128)} %bitcast.7), custom_call_target="tpu_custom_call" | custom-call | tf_op jit(solution)/shard_map/graph_layer/pallas_call | solution.py:558
  133.4 2.1 %hand_over.1 = (f32[4,128,256]{2,1,0:T(8,128)}, f32[256,256]{1,0:T(8,128)}, f32[4,128,256]{2,1,0:T(8,128)}) custom-call(f32[4,128,256]{2,1,0:T(8,128)} %get-tuple-element.9.refs_0_, f32[256,256]{1,0:T(8,128)} %get-tuple-element.10.refs_1_, f32[4,128,256]{2,1,0:T(8,128)} %get-tuple-element.11.refs_2_), custom_call_target="tpu_custom_call" | custom-call | tf_op jit(solution)/shard_map/hand_over/pallas_call | solution.py:576

commit v5 on v4

--- a/solution.py
+++ b/solution.py
@@ -325,17 +325,17 @@
 
     finish_gather(0)
     forward(0, next_half)
+    col_own[0].start()
     own[1].cross_left()
     xs[1][1].wait_recv()
     to_twin(1)(x_view(1, 1 - x_lo)(y, HA, 4))
     other[1].relay()
     own[1].cross_far()
     col_far[0].relay()
-    col_own[0].start()
     finish_gather(1)
-    sums = [send(col_far[0].finish(), CX.at[0], x_far)]
     col_own[0].relay()
     forward(1)
+    sums = [send(col_far[0].finish(), CX.at[0], x_far)]
     col_own[0].finish()
     col_far[1].relay()
     col_own[1].start()
@@ -458,13 +458,13 @@
     other[1].relay()
     own[1].cross_far()
     join(0, moves, 1)
+    row_own[0].start()
     for copy in w3:
         copy.wait_recv()
     mine_w = WO.at[pl.ds(pl.multiple_of(core * 128 + col * 16, 16), 16)]
     mine_w[...] = add_all(WS)
     w4 = [send(mine_w, mine_w, peer) for peer in col_peers]
     row_far[0].relay()
-    row_own[0].start()
     finish_back(1)
     moves = backward(1)
     row_own[0].relay()

time: 137 us -> 138 us (level)
    pallas_call x1, Pallas kernels: 133 us -> 134 us  [shards(): pl.pallas_call(lambda *refs: kernel(total_nodes, *refs), out_shape=out, i...]
where the time goes in v5:
time: 138 us; the launch traced here: 137 us
  Pallas kernels  136 us (99%)
    pallas_call x1, Pallas kernels, shards(): pl.pallas_call(lambda *refs: kernel(total_nodes, *refs), out_shape=out, i...  134 us

profile of v5, /device:TPU:0, one launch (start us, length us, event | category | flops | bytes accessed | tf_op | source)
XLA Modules:
  0.0 137.1 jit_solution(5667721142759437196)
XLA Ops:
  0.6 134.3 %graph_layer.1 = (f32[4,128,256]{2,1,0:T(8,128)}, f32[256,256]{1,0:T(8,128)}, f32[4,128,256]{2,1,0:T(8,128)}) custom-call(f32[4,128,256]{2,1,0:T(8,128)} %bitcast.8, f32[256,256]{1,0:T(8,128)} %refs_1_.1, f32[4,128,256]{2,1,0:T(8,128)} %bitcast.9, s32[1,96]{1,0:T(1,128)} %bitcast.10, s32[1,96]{1,0:T(1,128)} %bitcast.11, f32[96,128,128]{2,1,0:T(8,128)} %bitcast.7), custom_call_target="tpu_custom_call" | custom-call | tf_op jit(solution)/shard_map/graph_layer/pallas_call | solution.py:558
  135.0 2.1 %hand_over.1 = (f32[4,128,256]{2,1,0:T(8,128)}, f32[256,256]{1,0:T(8,128)}, f32[4,128,256]{2,1,0:T(8,128)}) custom-call(f32[4,128,256]{2,1,0:T(8,128)} %get-tuple-element.9.refs_0_, f32[256,256]{1,0:T(8,128)} %get-tuple-element.10.refs_1_, f32[4,128,256]{2,1,0:T(8,128)} %get-tuple-element.11.refs_2_), custom_call_target="tpu_custom_call" | custom-call | tf_op jit(solution)/shard_map/hand_over/pallas_call | solution.py:576
